TPU v7x, 128 devices: a whole 4x4x4 slice. The times are simulated.
128 devices in a mesh: row: 8 (over y, x_hi), col: 16 (over x_lo, z, core).
Axes of the slice: x: 4 (x_hi: 2, x_lo: 2; x = x_hi * 2 + x_lo), y: 4, z: 4, core: 2. Of those that a mesh axis runs over, the one named last changes fastest.
Arguments:
- cov: float32 [8192, 8192], P('row', 'col'), as said below
- obs_cells: int32 [3, 256], replicated, may hold values from 0 to 8191, as said below
- obs_var: float32 [3, 256], replicated, may hold values from 0.25 to 1
- wind: float32 [2, 64, 128], replicated, may hold values from -0.2 to 0.2
- diffusivity: float32 [64, 128], replicated, may hold values from 0.01 to 0.05
- noise: float32 [64, 128], replicated, may hold values from 0.05 to 0.5
Outputs:
- forecast: float32 [8192, 8192], P('row', 'col')
Inputs may be any that keep to these rules, and one draw needn't show every extreme that they name: `cov`: symmetric and positive definite. `obs_cells`: within each batch the 256 cells are distinct, and every batch observes cell 0 and cell 8192 - 1.
All inputs are finite; a program needn't handle non-finite values.
Results may differ from a plain program's by a relative error of at most 0.00013.
Values sent between devices are 32-bit elements; how exact they have to be, the bound alone decides.
No kernel may reach another device: no remote copies, remote signals or barrier semaphores. Data moves between devices by JAX's collectives and lax.ppermute only.
A program may use at most 64 MiB of HBM per device.

v0:
```python
import functools

import jax
import jax.numpy as jnp
from jax import lax
from jax.experimental import pallas as pl
from jax.experimental.pallas import tpu as pltpu
from jax.sharding import PartitionSpec as P


HI = lax.Precision.HIGHEST
F32 = jnp.float32
W = 128
ROWS = 8
COLS = 16
CAP_ROW = 128
CAP_COL = 72


def dot(a, b, dims=((1,), (0,)), precision=HI):
    return lax.dot_general(a, b, (dims, ((), ())), precision=precision, preferred_element_type=F32)


def recip(x):
    r = pltpu.reciprocal(x, approx=True)
    return r * (2.0 - x * r)


def lane_b(v, lane):
    return jnp.broadcast_to(v[:, lane : lane + 1], (8, 128))


def sub_b(v, sub):
    return jnp.broadcast_to(v[sub : sub + 1, :], (8, 128))


def invert_block(rows):
    lane = lax.broadcasted_iota(jnp.int32, (8, 128), 1)
    sub = lax.broadcasted_iota(jnp.int32, (8, 128), 0)
    rows = list(rows)
    for p in range(16):
        base = 8 * p
        panel = (lane >= base) & (lane < base + 8)
        src = rows[p]
        rb = [sub_b(src, i) for i in range(8)]
        e = [[lane_b(rb[i], base + j) if j >= i else None for j in range(8)] for i in range(8)]
        rb = [jnp.where(panel, jnp.where(lane == base + i, 1.0, 0.0), rb[i]) for i in range(8)]
        for k in range(8):
            r = recip(e[k][k])
            f = [e[i][k] if i < k else e[k][i] for i in range(8)]
            for j in range(k + 1, 8):
                e[k][j] = e[k][j] * r
            rb[k] = rb[k] * r
            for i in range(8):
                if i == k:
                    continue
                for j in range(max(i, k + 1), 8):
                    e[i][j] = e[i][j] - f[i] * e[k][j]
                rb[i] = rb[i] - f[i] * rb[k]
        for q in list(range(p + 1, 16)) + list(range(p)):
            t = rows[q]
            even = jnp.where(panel, 0.0, t)
            odd = None
            for j in range(8):
                m = lane_b(t, base + j) * rb[j]
                if j % 2 == 0:
                    even = even - m
                else:
                    odd = m if odd is None else odd + m
            rows[q] = even - odd
        out = rb[0]
        for i in range(1, 8):
            out = jnp.where(sub == i, rb[i], out)
        rows[p] = out
    return rows


def eliminate(o_ref, d_ref, y_ref, n):
    blocks = n // W

    def save(block):
        rows = invert_block([block[8 * q : 8 * q + 8, :] for q in range(16)])
        return jnp.concatenate(rows, axis=0)

    def step(kb, ahead):
        blk = pl.ds(pl.multiple_of(kb * W, W), W)
        dinv = d_ref[...]
        if ahead:
            nxt = pl.ds(pl.multiple_of(jnp.where(kb == blocks, 0, kb + 1) * W, W), W)
            following = save(o_ref[nxt, nxt] - dot(o_ref[nxt, blk], dot(dinv, o_ref[blk, nxt])))
        col = o_ref[:, blk]
        y_ref[...] = dot(dinv, o_ref[blk, :])
        y_ref[:, blk] = dinv
        o_ref[:, blk] = jnp.zeros((n + W, W), F32)
        o_ref[...] = o_ref[...] - dot(col, y_ref[...])
        o_ref[blk, :] = y_ref[...]
        if ahead:
            d_ref[...] = following

    def body(trip, carry):
        step(jnp.where(trip == 0, blocks, trip - 1), True)
        return carry

    d_ref[...] = jnp.zeros((W, W), F32)
    o_ref[n:, :] = jnp.zeros((W, n + W), F32)
    o_ref[:, n:] = jnp.zeros((n + W, W), F32)
    lax.fori_loop(0, blocks, body, 0)
    step(blocks - 1, False)


def put_rows(full_ref, at, pieces_ref, j):
    for g in range(full_ref.shape[0]):
        full_ref[g, at, :] = pieces_ref[j, :, W * g : W * g + W]


def flat(full_ref, rows):
    return jnp.concatenate([full_ref[g, rows, :] for g in range(full_ref.shape[0])], axis=1)


def pack_pairs(core, offs_ref, own_ref, other_ref, full_ref, cap):
    def body(j, carry):
        for k in range(2):
            at = pl.ds(offs_ref[2 * j + k], cap)

            @pl.when(core == k)
            def _():
                put_rows(full_ref, at, own_ref, j)

            @pl.when(core != k)
            def _():
                put_rows(full_ref, at, other_ref, j)

        return carry

    lax.fori_loop(0, 8, body, 0)


def inverse_kernel(
    offs_ref, core_ref, own_ref, other_ref, var_ref, o_ref, full_ref, s_ref, d_ref, y_ref, *, n, cap
):
    pack_pairs(core_ref[0], offs_ref, own_ref, other_ref, full_ref, cap)
    diag = lax.broadcasted_iota(jnp.int32, (W, W), 1) == lax.broadcasted_iota(jnp.int32, (W, W), 0)

    def body(g, carry):
        at = pl.ds(pl.multiple_of(W * g, W), W)
        s_ref[at, 0:n] = flat(full_ref, at)
        s_ref[at, at] = s_ref[at, at] + jnp.where(diag, var_ref[0:1, at], 0.0)
        return carry

    lax.fori_loop(0, n // W, body, 0)
    eliminate(s_ref, d_ref, y_ref, n)
    o_ref[...] = s_ref[0:n, 0:n]


VM = pl.BlockSpec(memory_space=pltpu.VMEM)
SM = pl.BlockSpec(memory_space=pltpu.SMEM)


def inverse(offs, core, own, other, variances):
    n = variances.shape[0]
    cap = own.shape[1]
    return pl.pallas_call(
        functools.partial(inverse_kernel, n=n, cap=cap),
        out_shape=jax.ShapeDtypeStruct((n, n), F32),
        in_specs=[SM, SM, VM, VM, VM],
        out_specs=VM,
        scratch_shapes=[
            pltpu.VMEM((n // W, n + cap, W), F32),
            pltpu.VMEM((n + W, n + W), F32),
            pltpu.VMEM((W, W), F32),
            pltpu.VMEM((W, n + W), F32),
        ],
        name="inverse",
    )(offs, core, own, other, jnp.broadcast_to(variances[None, :], (8, n)))


def select_kernel(ridx_ref, cidx_ref, cov_ref, x_ref, y_ref, c_ref):
    for i in range(x_ref.shape[0]):
        x_ref[i : i + 1, :] = cov_ref[pl.ds(ridx_ref[i], 1), :]
    lanes = lax.broadcasted_iota(jnp.int32, (y_ref.shape[0], cov_ref.shape[1]), 1)
    pick = jnp.where(lanes == cidx_ref[...], 1.0, 0.0)
    corner = dot(pick, x_ref[...], ((1,), (1,)))
    for k in range(c_ref.shape[0]):
        c_ref[k] = corner
    pick_columns(pick, cov_ref, y_ref)


def pick_columns(pick, mat_ref, o_ref):
    def body(g, carry):
        at = pl.ds(pl.multiple_of(2 * W * g, 2 * W), 2 * W)
        o_ref[:, at] = dot(pick, mat_ref[at, :], ((1,), (1,)))
        return carry

    lax.fori_loop(0, mat_ref.shape[0] // (2 * W), body, 0)


def pick_kernel(cidx_ref, mat_ref, o_ref):
    step = 96

    def body(g, carry):
        at = pl.ds(pl.multiple_of(step * g, 8), step)
        lanes = lax.broadcasted_iota(jnp.int32, (step, mat_ref.shape[1]), 1)
        pick = jnp.where(lanes == cidx_ref[at, :], 1.0, 0.0)
        pick_columns(pick, mat_ref, o_ref.at[at, :])
        return carry

    lax.fori_loop(0, o_ref.shape[0] // step, body, 0)


def picked(cidx, mat):
    return pl.pallas_call(
        pick_kernel,
        out_shape=jax.ShapeDtypeStruct((cidx.shape[0], mat.shape[0]), F32),
        in_specs=[VM, VM],
        out_specs=VM,
        name="picked",
    )(cidx[:, None], mat)


def select(ridx, cidx, cov):
    rows, cols = cov.shape
    return pl.pallas_call(
        select_kernel,
        out_shape=(
            jax.ShapeDtypeStruct((ridx.shape[0], cols), F32),
            jax.ShapeDtypeStruct((cidx.shape[0], rows), F32),
            jax.ShapeDtypeStruct((8, cidx.shape[0], ridx.shape[0]), F32),
        ),
        in_specs=[SM, VM, VM],
        out_specs=(VM, VM, VM),
        name="select",
    )(ridx, cidx[:, None], cov)


def widen_kernel(slot_ref, p_ref, o_ref):
    n = o_ref.shape[2]
    lanes = lax.broadcasted_iota(jnp.int32, (p_ref.shape[2], n), 1)

    def body(r, total):
        put = jnp.where(lanes == slot_ref[r], 1.0, 0.0)
        return total + dot(p_ref[r], put)

    total = lax.fori_loop(0, p_ref.shape[0], body, jnp.zeros((p_ref.shape[1], n), F32))
    for k in range(o_ref.shape[0]):
        o_ref[k] = total


def widen(slots, pieces, n):
    return pl.pallas_call(
        widen_kernel,
        out_shape=jax.ShapeDtypeStruct((8, pieces.shape[1], n), F32),
        in_specs=[VM, VM],
        out_specs=VM,
        name="widen",
    )(slots[:, :, None], pieces)


def final_kernel(
    roffs_ref, coffs_ref, row_ref, core_ref, inv_ref, x0, x1, x2, x3, own_ref, other_ref, prior_ref,
    o_ref, xs_ref, ys_ref, gain_ref,
):
    n = inv_ref.shape[0]
    pairs = (x0, x1, x2, x3)
    row = row_ref[0]

    def pack(b, carry):
        for k, pair in enumerate(pairs):

            @pl.when((row // 2 - b) % len(pairs) == k)
            def _():
                for h in range(2):
                    at = pl.ds(roffs_ref[2 * b + h], pair.shape[1])
                    put_rows(xs_ref, at, pair, (row - h) % 2)

        return carry

    lax.fori_loop(0, len(pairs), pack, 0)
    pack_pairs(core_ref[0], coffs_ref, own_ref, other_ref, ys_ref, own_ref.shape[1])
    gain_ref[...] = dot(inv_ref[...], flat(xs_ref, slice(0, n)))
    per = 2

    def body(g, carry):
        cells = jnp.concatenate([ys_ref[per * g + i, 0:n, :] for i in range(per)], axis=1)
        at = pl.ds(pl.multiple_of(per * W * g, W), per * W)
        o_ref[at, :] = prior_ref[at, :] - dot(cells, gain_ref[...], ((0,), (0,)))
        return carry

    lax.fori_loop(0, o_ref.shape[0] // (per * W), body, 0)


def final(roffs, coffs, row, core, inv, pairs, own, other, prior):
    n = inv.shape[0]
    return pl.pallas_call(
        final_kernel,
        out_shape=jax.ShapeDtypeStruct(prior.shape, F32),
        in_specs=[SM, SM, SM, SM] + [VM] * 8,
        out_specs=VM,
        scratch_shapes=[
            pltpu.VMEM((prior.shape[1] // W, n + pairs[0].shape[1], W), F32),
            pltpu.VMEM((prior.shape[0] // W, n + own.shape[1], W), F32),
            pltpu.VMEM((n, prior.shape[1]), F32),
        ],
        name="update",
    )(roffs, coffs, row, core, inv, *pairs, own, other, prior)


def stencil_table(wind, diffusivity):
    east_wind = wind[0]
    north_wind = wind[1]
    from_west = diffusivity + jnp.maximum(east_wind, 0.0)
    from_east = diffusivity + jnp.maximum(-east_wind, 0.0)
    from_north = diffusivity + jnp.maximum(north_wind, 0.0)
    from_south = diffusivity + jnp.maximum(-north_wind, 0.0)
    center = 1.0 - (from_west + from_east + from_north + from_south)
    x = lax.broadcasted_iota(jnp.int32, from_west.shape, 1)
    from_west = jnp.where(x > 0, from_west, 0.0)
    from_east = jnp.where(x < W - 1, from_east, 0.0)
    return jnp.stack([center, from_west, from_east, from_north, from_south])


def lane_pass(segs, w_ref, first):
    out = []
    for g in range(1, len(segs) - 1):
        at = slice(first + g, first + g + 1)
        v = segs[g]
        out.append(
            w_ref[0, at, :] * v
            + w_ref[1, at, :] * pltpu.roll(v, 1, 1)
            + w_ref[2, at, :] * pltpu.roll(v, W - 1, 1)
            + w_ref[3, at, :] * segs[g - 1]
            + w_ref[4, at, :] * segs[g + 1]
        )
    return out


def cols_kernel(w_ref, b_ref, low_ref, high_ref, o_ref, *, step):
    copies = o_ref.shape[0] if len(o_ref.shape) == 3 else 0

    def body(t, carry):
        at = pl.ds(pl.multiple_of(step * t, 8), step)
        segs = [low_ref[at, 0:W], low_ref[at, W : 2 * W]]
        segs += [b_ref[at, W * g : W * g + W] for g in range(b_ref.shape[1] // W)]
        segs += [high_ref[at, 0:W], high_ref[at, W : 2 * W]]
        segs = lane_pass(lane_pass(segs, w_ref, 0), w_ref, 1)
        for g, v in enumerate(segs):
            lanes = slice(W * g, W * g + W)
            if copies:
                for k in range(copies):
                    o_ref[k, at, lanes] = v
            else:
                o_ref[at, lanes] = v
        return carry

    lax.fori_loop(0, b_ref.shape[0] // step, body, 0)


def twice_cols(weights, block, low, high, copies=0):
    step = 24 if block.shape[0] % 64 else 64
    shape = ((copies,) if copies else ()) + block.shape
    return pl.pallas_call(
        functools.partial(cols_kernel, step=step),
        out_shape=jax.ShapeDtypeStruct(shape, F32),
        in_specs=[VM, VM, VM, VM],
        out_specs=VM,
        name="stencil_lanes",
    )(weights, block, low, high)


def rows_kernel(w_ref, b_ref, low_ref, high_ref, o_ref, mid_ref):
    n = b_ref.shape[0] // W
    cols = b_ref.shape[1]

    def coef(k, g):
        return jnp.broadcast_to(w_ref[g, :, k : k + 1], (W, cols))

    def one(v, north, south, g):
        return (
            coef(0, g) * v
            + coef(1, g) * pltpu.roll(v, 1, 0)
            + coef(2, g) * pltpu.roll(v, W - 1, 0)
            + coef(3, g) * north
            + coef(4, g) * south
        )

    def src(g):
        if g < 2:
            return low_ref[W * g : W * g + W, :]
        if g < n + 2:
            return b_ref[W * (g - 2) : W * (g - 2) + W, :]
        return high_ref[W * (g - n - 2) : W * (g - n - 2) + W, :]

    def first(g):
        mid_ref[pl.ds(pl.multiple_of(W * (g - 1), W), W), :] = one(
            src(g), src(g - 1), src(g + 1), g
        )

    def inner(g, carry):
        at = pl.multiple_of(W * (g - 2), W)
        v = b_ref[pl.ds(at, W), :]
        mid_ref[pl.ds(at + W, W), :] = one(v, b_ref[pl.ds(at - W, W), :], b_ref[pl.ds(at + W, W), :], g)
        return carry

    def second(g, carry):
        m = pl.multiple_of(W * (g - 1), W)
        o_ref[pl.ds(m - W, W), :] = one(
            mid_ref[pl.ds(m, W), :], mid_ref[pl.ds(m - W, W), :], mid_ref[pl.ds(m + W, W), :], g
        )
        return carry

    for g in (1, 2, n + 1, n + 2):
        first(g)
    lax.fori_loop(3, n + 1, inner, 0)
    lax.fori_loop(2, n + 2, second, 0)


def twice_rows(weights, block, low, high):
    return pl.pallas_call(
        rows_kernel,
        out_shape=jax.ShapeDtypeStruct(block.shape, F32),
        in_specs=[VM, VM, VM, VM],
        out_specs=VM,
        scratch_shapes=[pltpu.VMEM((block.shape[0] + 2 * W, block.shape[1]), F32)],
        name="stencil_rows",
    )(weights, block, low, high)


def prior_kernel(gap_ref, w_ref, wr_ref, noise_ref, b_ref, low_ref, high_ref, o_ref, mid_ref):
    nseg = b_ref.shape[1] // W
    lane = lax.broadcasted_iota(jnp.int32, (W, W), 1)
    sub = lax.broadcasted_iota(jnp.int32, (W, W), 0)
    step = 32

    def body(t, carry):
        base = pl.multiple_of(W * t, W)
        for h in range(W // step):
            at = pl.ds(base + step * h, step)
            segs = [low_ref[at, 0:W], low_ref[at, W : 2 * W]]
            segs += [b_ref[at, W * g : W * g + W] for g in range(nseg)]
            segs += [high_ref[at, 0:W], high_ref[at, W : 2 * W]]
            for g, v in enumerate(lane_pass(segs, w_ref, 0)):
                mid_ref[g, step * h : step * h + step, :] = v
        ahead = gap_ref[0] + 1 - t
        for g in range(nseg + 2):

            @pl.when(jnp.abs(ahead + g) <= 1)
            def _():
                here = W * (ahead + g) + lane - sub
                coef = [jnp.broadcast_to(wr_ref[t + 2, :, k : k + 1], (W, W)) for k in range(5)]
                spread = jnp.where(here == 0, coef[0], 0.0)
                spread = jnp.where(here == -1, coef[1], spread)
                spread = jnp.where(here == 1, coef[2], spread)
                spread = jnp.where(here == -W, coef[3], spread)
                spread = jnp.where(here == W, coef[4], spread)
                mid_ref[g] = mid_ref[g] + spread * noise_ref[g + 1 : g + 2, :]

        for h in range(W // step):
            at = pl.ds(base + step * h, step)
            mid = [mid_ref[g, step * h : step * h + step, :] for g in range(nseg + 2)]
            for g, v in enumerate(lane_pass(mid, w_ref, 1)):
                o_ref[at, W * g : W * g + W] = v
        for g in range(nseg):

            @pl.when(ahead + g + 1 == 0)
            def _():
                at = pl.ds(base, W)
                lanes = slice(W * g, W * g + W)
                last = jnp.where(lane == sub, noise_ref[g + 2 : g + 3, :], 0.0)
                o_ref[at, lanes] = o_ref[at, lanes] + last

        return carry

    lax.fori_loop(0, o_ref.shape[0] // W, body, 0)


def prior_cols(gap, weights, row_weights, noise, block, low, high):
    return pl.pallas_call(
        prior_kernel,
        out_shape=jax.ShapeDtypeStruct(block.shape, F32),
        in_specs=[SM, VM, VM, VM, VM, VM, VM],
        out_specs=VM,
        scratch_shapes=[pltpu.VMEM((block.shape[1] // W + 2, W, W), F32)],
        name="prior_lanes",
    )(gap, weights, row_weights, noise, block, low, high)


def halos(block, axis, dim, width):
    count = lax.axis_size(axis)
    forward = [(i, i + 1) for i in range(count - 1)]
    backward = [(target, source) for source, target in forward]
    low = lax.ppermute(
        lax.slice_in_dim(block, block.shape[dim] - width, None, axis=dim), axis, forward
    )
    high = lax.ppermute(lax.slice_in_dim(block, 0, width, axis=dim), axis, backward)
    return low, high


def gather_sum(parts, axis):
    count = lax.axis_size(axis)
    size = parts.shape[0] // count
    pieces = lax.all_to_all(parts.reshape(count, size, -1), axis, 0, 0)
    mine = jnp.sum(pieces, axis=0)
    full = lax.all_to_all(jnp.broadcast_to(mine[None], (count,) + mine.shape), axis, 0, 0)
    return full.reshape(parts.shape)


def share(copies, axis, groups=None):
    return lax.all_to_all(copies, axis, 0, 0, axis_index_groups=groups)


def windows(array, cap, count):
    size = array.shape[0] // count
    padded = jnp.pad(array, ((0, cap), (0, 0)))
    return jnp.stack([padded[size * i : size * i + cap] for i in range(count)])


def local(cov, obs_cells, obs_var, wind, diffusivity, noise):
    rows_here, cols_here = cov.shape
    row = lax.axis_index("row")
    col = lax.axis_index("col")
    row_start = row * rows_here
    col_start = col * cols_here
    core = (col % 2)[None]
    same_core = [[c for c in range(COLS) if c % 2 == k] for k in range(2)]
    swap = [(c, c ^ 1) for c in range(COLS)]

    cells = obs_cells.reshape(-1)
    n = cells.shape[0]
    ids = jnp.arange(n, dtype=jnp.int32)
    key = (cells // cols_here) * n + ids
    place = jnp.sum((key[None, :] < key[:, None]).astype(jnp.int32), axis=1)
    at = place[:, None] == ids[None, :]
    ordered = jnp.sum(jnp.where(at, cells[:, None], 0), axis=0)
    variances = jnp.sum(jnp.where(at, obs_var.reshape(-1)[:, None], 0.0), axis=0)
    edges = jnp.arange(COLS + 1, dtype=jnp.int32) * cols_here
    bounds = jnp.sum((cells[None, :] < edges[:, None]).astype(jnp.int32), axis=1)
    col_offs = bounds[:-1]
    row_bounds = bounds[:: COLS // ROWS]
    row_offs = row_bounds[:-1]
    row_counts = row_bounds[1:] - row_bounds[:-1]
    fits = (jnp.max(row_counts) <= CAP_ROW) & (jnp.max(bounds[1:] - bounds[:-1]) <= CAP_COL)

    padded = jnp.pad(ordered, (0, CAP_ROW))
    ridx = lax.dynamic_slice_in_dim(padded, row_offs[row], CAP_ROW) - row_start
    cidx = lax.dynamic_slice_in_dim(padded, col_offs[col], CAP_COL) - col_start
    ridx = jnp.clip(ridx, 0, rows_here - 1)
    cidx = jnp.clip(cidx, 0, cols_here - 1)
    lanes = jnp.arange(CAP_ROW, dtype=jnp.int32)[None, :]
    slots = jnp.where(lanes < row_counts[:, None], row_offs[:, None] + lanes, -1)

    margin = 2 * W
    grid_row = row_start // W
    grid_col = col_start // W
    table = jnp.pad(stencil_table(wind, diffusivity), ((0, 0), (2, 2), (0, 0)))
    row_w = lax.dynamic_slice_in_dim(table, grid_row, rows_here // W + 4, 1)
    col_w = lax.dynamic_slice_in_dim(table, grid_col, cols_here // W + 4, 1)
    noise_cols = lax.dynamic_slice_in_dim(
        jnp.pad(noise, ((2, 2), (0, 0))), grid_col, cols_here // W + 4, 0
    )
    row_sub = jnp.transpose(row_w, (1, 2, 0))

    xg, yg, cg = select(ridx, cidx, cov)
    c_pieces = share(cg, "row")
    row_halo = halos(cov, "row", 0, margin)
    y_halo = halos(yg, "row", 1, margin)
    c_rows = widen(slots, c_pieces, n)
    c_own = share(c_rows, "col", same_core)
    c_other = lax.ppermute(c_own, "col", swap)

    tall = twice_rows(row_sub, cov, *row_halo)
    col_halo = halos(tall, "col", 1, margin)
    gap = (grid_col - 2 - grid_row)[None]
    prior = prior_cols(gap, col_w, row_sub, noise_cols, tall, *col_halo)

    x_halo = halos(xg, "col", 1, margin)
    vx = twice_cols(col_w, xg, *x_halo)
    vy = twice_cols(row_w, yg, *y_halo, copies=8)
    pair = jnp.stack([vx, lax.ppermute(vx, "row", [(i, i ^ 1) for i in range(ROWS)])])
    pairs = (pair,) + tuple(
        lax.ppermute(pair, "row", [(i, (i + 2 * k) % ROWS) for i in range(ROWS)])
        for k in range(1, ROWS // 2)
    )
    y_own = share(vy, "col", same_core)
    y_other = lax.ppermute(y_own, "col", swap)

    blocks = jnp.arange(ROWS, dtype=jnp.int32)

    def long_x():
        hit = (ordered >= row_start) & (ordered < row_start + rows_here)
        part = cov[jnp.clip(ordered - row_start, 0, rows_here - 1), :]
        return gather_sum(jnp.where(hit[:, None], part, 0.0), "row")

    def cores(array):
        parts = windows(array, CAP_COL, COLS)
        parts = parts.reshape((COLS // 2, 2) + parts.shape[1:])
        return tuple(
            lax.dynamic_index_in_dim(parts, k, 1, keepdims=False) for k in (core[0], 1 - core[0])
        )

    even_cols = jnp.arange(COLS, dtype=jnp.int32) * (n // COLS)
    even_rows = blocks * (n // ROWS)

    def long_corner():
        own, other = cores(gather_sum(picked(ordered - col_start, long_x()), "col"))
        return even_cols, own, other

    def long_update():
        x = long_x()
        y = gather_sum(picked(ordered - col_start, cov), "col")
        x = twice_cols(col_w, x, *halos(x, "col", 1, margin))
        y = twice_cols(row_w, y, *halos(y, "row", 1, margin))
        pieces = windows(x, CAP_ROW, ROWS).reshape((ROWS // 2, 2, CAP_ROW, -1))
        pieces = jnp.stack(
            [lax.dynamic_index_in_dim(pieces, (row + k) % 2, 1, keepdims=False) for k in range(2)], 1
        )
        sets = tuple(
            lax.dynamic_index_in_dim(pieces, (row // 2 - k) % (ROWS // 2), 0, keepdims=False)
            for k in range(ROWS // 2)
        )
        return (even_rows, even_cols, sets) + cores(y)

    def unless(fits, short, long):
        def body(state):
            return jnp.bool_(False), long()

        return lax.while_loop(lambda state: state[0], body, (~fits, short))[1]

    c_offs, c_own, c_other = unless(fits, (col_offs, c_own, c_other), long_corner)
    inv = inverse(c_offs, core, c_own, c_other, variances)
    x_offs, y_offs, pairs, y_own, y_other = unless(
        fits, (row_offs, col_offs, pairs, y_own, y_other), long_update
    )
    return final(x_offs, y_offs, row[None], core, inv, pairs, y_own, y_other, prior)


def solution(mesh):
    placed = (P("row", "col"), P(), P(), P(), P(), P())

    return jax.shard_map(
        local, mesh=mesh, in_specs=placed, out_specs=P("row", "col"), check_vma=False
    )
```

profile of v0, /device:TPU:19, one launch (start us, length us, event | category | flops | bytes accessed | tf_op | source)
XLA Modules:
  0.0 245.6 jit_solution(15489672040111276810)
XLA Ops:
  9.9 5.6 %select.63 = (f32[128,512]{1,0:T(8,128)}, f32[72,1024]{1,0:T(8,128)}, f32[8,72,128]{2,1,0:T(8,128)}) custom-call(s32[128]{0:T(128)} %fusion.65.ridx_ref, s32[72,1]{1,0:T(8,128)} %copy.90.cidx_ref, f32[1024,512]{1,0:T(8,128)} %b_ref.1), custom_call_target="tpu_custom_call" | custom-call | tf_op jit(solution)/shard_map/select/pallas_call | solution.py:222
  15.5 5.8 %all-to-all-start.9 = ((f32[8,72,128]{2,1,0:T(8,128)}), f32[8,72,128]{2,1,0:T(8,128)S(1)}, u32[]{:S(2)}, u32[]{:S(2)}) async-start(f32[8,72,128]{2,1,0:T(8,128)} %get-tuple-element.157), calls=%async_computation.9 | async-start | bytes 589824 | tf_op jit(solution)/shard_map/all_to_all | solution.py:507
  22.3 4.7 %all-to-all-done.9.p_ref = f32[8,72,128]{2,1,0:T(8,128)S(1)} async-done(((f32[8,72,128]{2,1,0:T(8,128)}), f32[8,72,128]{2,1,0:T(8,128)S(1)}, u32[]{:S(2)}, u32[]{:S(2)}) %all-to-all-start.9) | async-done | bytes 294944 | tf_op jit(solution)/shard_map/all_to_all | solution.py:507
  27.7 5.9 %widen.1 = f32[8,72,768]{2,1,0:T(8,128)} custom-call(s32[8,128,1]{2,1,0:T(8,128)} %add_select_fusion.slot_ref, f32[8,72,128]{2,1,0:T(8,128)} %copy-done.9), custom_call_target="tpu_custom_call" | custom-call | tf_op jit(solution)/shard_map/widen/pallas_call | solution.py:249
  33.7 6.4 %all-to-all-start.10 = ((f32[8,72,768]{2,1,0:T(8,128)}), f32[8,72,768]{2,1,0:T(8,128)}, u32[]{:S(2)}, u32[]{:S(2)}) async-start(f32[8,72,768]{2,1,0:T(8,128)} %widen.1), calls=%async_computation.10 | async-start | bytes 3538944 | tf_op jit(solution)/shard_map/all_to_all | solution.py:507
  40.0 2.5 %collective-permute-start.10 = (f32[72,256]{1,0:T(8,128)S(1)}, f32[72,256]{1,0:T(8,128)S(1)}, u32[]{:S(2)}, u32[]{:S(2)}) collective-permute-start(f32[72,256]{1,0:T(8,128)S(1)} %get-tuple-element.424), channel_id=1, source_target_pairs={{0,16},{16,32},{32,48},{48,64},{64,80},{80,96},{96,112},{1,17},{17... | collective-permute-start | bytes 221192 | tf_op jit(solution)/shard_map/ppermute | solution.py:490
  42.5 5.2 %collective-permute-start.11 = (f32[72,256]{1,0:T(8,128)S(1)}, f32[72,256]{1,0:T(8,128)S(1)}, u32[]{:S(2)}, u32[]{:S(2)}) collective-permute-start(f32[72,256]{1,0:T(8,128)S(1)} %get-tuple-element.423), channel_id=1, source_target_pairs={{16,0},{32,16},{48,32},{64,48},{80,64},{96,80},{112,96},{17,1},{33... | collective-permute-start | bytes 221192 | tf_op jit(solution)/shard_map/ppermute | solution.py:493
  47.9 2.7 %copy.89 = f32[5,64,128]{0,2,1:T(8,128)} copy(f32[5,64,128]{2,1,0:T(8,128)S(1)} %bitcast_dynamic-update-slice_fusion) | data formatting | bytes 327680 | tf_op jit(solution)/shard_map/stack | solution.py:318
  52.1 10.1 %collective-permute-done.10.low_ref = f32[72,256]{1,0:T(8,128)S(1)} collective-permute-done((f32[72,256]{1,0:T(8,128)S(1)}, f32[72,256]{1,0:T(8,128)S(1)}, u32[]{:S(2)}, u32[]{:S(2)}) %collective-permute-start.10) | collective-permute-done | bytes 73760 | tf_op jit(solution)/shard_map/ppermute | solution.py:490
  63.5 3.2 %stencil_lanes.5 = f32[8,72,1024]{2,1,0:T(8,128)} custom-call(f32[5,12,128]{2,1,0:T(8,128)S(1)} %copy.92.w_ref, f32[72,1024]{1,0:T(8,128)} %get-tuple-element.154.b_ref, f32[72,256]{1,0:T(8,128)} %copy-done.19, f32[72,256]{1,0:T(8,128)} %copy-done.20), custom_call_target="tpu_custom_call" | custom-call | tf_op jit(solution)/shard_map/stencil_lanes/pallas_call | solution.py:360
  66.7 5.2 %all-to-all-start.8 = ((f32[8,72,1024]{2,1,0:T(8,128)}), f32[8,72,1024]{2,1,0:T(8,128)}, u32[]{:S(2)}, u32[]{:S(2)}) async-start(f32[8,72,1024]{2,1,0:T(8,128)} %stencil_lanes.5), calls=%async_computation.8 | async-start | bytes 4718592 | tf_op jit(solution)/shard_map/all_to_all | solution.py:507
  72.0 3.5 %collective-permute-start.14 = (f32[256,512]{1,0:T(8,128)S(1)}, f32[256,512]{1,0:T(8,128)S(1)}, u32[]{:S(2)}, u32[]{:S(2)}) collective-permute-start(f32[256,512]{1,0:T(8,128)S(1)} %get-tuple-element.422), channel_id=1, source_target_pairs={{0,16},{16,32},{32,48},{48,64},{64,80},{80,96},{96,112},{1,17},{17... | collective-permute-start | bytes 1572872 | tf_op jit(solution)/shard_map/ppermute | solution.py:490
  75.5 4.2 %collective-permute-start.15 = (f32[256,512]{1,0:T(8,128)S(1)}, f32[256,512]{1,0:T(8,128)S(1)}, u32[]{:S(2)}, u32[]{:S(2)}) collective-permute-start(f32[256,512]{1,0:T(8,128)S(1)} %get-tuple-element.421), channel_id=1, source_target_pairs={{16,0},{32,16},{48,32},{64,48},{80,64},{96,80},{112,96},{17,1},{33... | collective-permute-start | bytes 1572872 | tf_op jit(solution)/shard_map/ppermute | solution.py:493
  79.7 4.8 %collective-permute-start.13 = (f32[8,72,768]{2,1,0:T(8,128)}, f32[8,72,768]{2,1,0:T(8,128)}, u32[]{:S(2)}, u32[]{:S(2)}) collective-permute-start(f32[8,72,768]{2,1,0:T(8,128)} %all-to-all-done.10), channel_id=1, source_target_pairs={{0,1},{1,0},{2,3},{3,2},{4,5},{5,4},{6,7},{7,6},{8,9},{9,8},{10,11... | collective-permute-start | bytes 5308424 | tf_op jit(solution)/shard_map/ppermute | solution.py:567
  84.5 2.1 fusion.74.w_ref.wr_ref
  86.6 20.6 %collective-permute-done.14.low_ref = f32[256,512]{1,0:T(8,128)S(1)} collective-permute-done((f32[256,512]{1,0:T(8,128)S(1)}, f32[256,512]{1,0:T(8,128)S(1)}, u32[]{:S(2)}, u32[]{:S(2)}) %collective-permute-start.14) | collective-permute-done | bytes 524320 | tf_op jit(solution)/shard_map/ppermute | solution.py:490
  107.1 11.5 %collective-permute-done.15.high_ref = f32[256,512]{1,0:T(8,128)S(1)} collective-permute-done((f32[256,512]{1,0:T(8,128)S(1)}, f32[256,512]{1,0:T(8,128)S(1)}, u32[]{:S(2)}, u32[]{:S(2)}) %collective-permute-start.15) | collective-permute-done | bytes 524320 | tf_op jit(solution)/shard_map/ppermute | solution.py:493
  119.5 5.9 %stencil_rows.1.b_ref = f32[1024,512]{1,0:T(8,128)} custom-call(f32[12,128,5]{2,1,0:T(8,128)} %fusion.74.w_ref.wr_ref, f32[1024,512]{1,0:T(8,128)S(1)} %copy-done, f32[256,512]{1,0:T(8,128)} %copy-done.15, f32[256,512]{1,0:T(8,128)} %copy-done.16), custom_call_target="tpu_custom_call" | custom-call | tf_op jit(solution)/shard_map/stencil_rows/pallas_call | solution.py:417
  125.4 3.2 %fusion.69 = (f32[1024,256]{1,0:T(8,128)}, f32[1024,256]{1,0:T(8,128)}) fusion(f32[1024,512]{1,0:T(8,128)} %stencil_rows.1.b_ref), kind=kLoop, calls=%fused_computation.170 | loop fusion | bytes 4194304 | tf_op jit(solution)/shard_map/slice | solution.py:493
  128.5 7.5 %collective-permute-start.16 = (f32[1024,256]{1,0:T(8,128)}, f32[1024,256]{1,0:T(8,128)}, u32[]{:S(2)}, u32[]{:S(2)}) collective-permute-start(f32[1024,256]{1,0:T(8,128)} %get-tuple-element.420), channel_id=1, source_target_pairs={{0,1},{1,2},{2,3},{3,4},{4,5},{5,6},{6,7},{7,8},{8,9},{9,10},{10,1... | collective-permute-start | bytes 3145736 | tf_op jit(solution)/shard_map/ppermute | solution.py:490
  136.0 1.9 collective-permute-start.17
  138.0 3.6 %collective-permute-start.4 = (f32[128,256]{1,0:T(8,128)S(1)}, f32[128,256]{1,0:T(8,128)S(1)}, u32[]{:S(2)}, u32[]{:S(2)}) collective-permute-start(f32[128,256]{1,0:T(8,128)S(1)} %get-tuple-element.426), channel_id=1, source_target_pairs={{0,1},{1,2},{2,3},{3,4},{4,5},{5,6},{6,7},{7,8},{8,9},{9,10},{10,1... | collective-permute-start | bytes 393224 | tf_op jit(solution)/shard_map/ppermute | solution.py:490
  141.6 3.0 %collective-permute-start.5 = (f32[128,256]{1,0:T(8,128)S(1)}, f32[128,256]{1,0:T(8,128)S(1)}, u32[]{:S(2)}, u32[]{:S(2)}) collective-permute-start(f32[128,256]{1,0:T(8,128)S(1)} %get-tuple-element.425), channel_id=1, source_target_pairs={{1,0},{2,1},{3,2},{4,3},{5,4},{6,5},{7,6},{8,7},{9,8},{10,9},{11,1... | collective-permute-start | bytes 393224 | tf_op jit(solution)/shard_map/ppermute | solution.py:493
  147.8 1.6 collective-permute-done.4.low_ref
  149.3 4.4 %collective-permute-done.5.high_ref = f32[128,256]{1,0:T(8,128)S(1)} collective-permute-done((f32[128,256]{1,0:T(8,128)S(1)}, f32[128,256]{1,0:T(8,128)S(1)}, u32[]{:S(2)}, u32[]{:S(2)}) %collective-permute-start.5) | collective-permute-done | bytes 131104 | tf_op jit(solution)/shard_map/ppermute | solution.py:493
  154.4 2.2 stencil_lanes.4
  158.3 6.9 %collective-permute-done.6 = f32[128,512]{1,0:T(8,128)S(1)} collective-permute-done((f32[128,512]{1,0:T(8,128)}, f32[128,512]{1,0:T(8,128)S(1)}, u32[]{:S(2)}, u32[]{:S(2)}) %collective-permute-start.6) | collective-permute-done | bytes 262176 | tf_op jit(solution)/shard_map/ppermute | solution.py:577
  167.7 1.6 collective-permute-start.9
  169.3 10.5 %prior_lanes.1.prior_ref = f32[1024,512]{1,0:T(8,128)} custom-call(s32[1]{0:T(128)} %bitcast.16.gap_ref, f32[5,8,128]{2,1,0:T(8,128)S(1)} %copy.91.w_ref, f32[12,128,5]{2,1,0:T(8,128)} %fusion.74.w_ref.wr_ref, f32[8,128]{1,0:T(8,128)} %pad_dynamic-slice_fusion.10.noise_ref, f32[1024,512]{1,0:T(8,128)} %stencil_rows.1.b_ref, ...), custom_call_target="tpu_custom_call" | custom-call | tf_op jit(solution)/shard_map/prior_lanes/pallas_call | solution.py:476
  179.8 2.6 %collective-permute-start.12 = (f32[8,72,1024]{2,1,0:T(8,128)}, f32[8,72,1024]{2,1,0:T(8,128)}, u32[]{:S(2)}, u32[]{:S(2)}) collective-permute-start(f32[8,72,1024]{2,1,0:T(8,128)} %all-to-all-done.8), channel_id=1, source_target_pairs={{0,1},{1,0},{2,3},{3,2},{4,5},{5,4},{6,7},{7,6},{8,9},{9,8},{10,11... | collective-permute-start | bytes 7077896 | tf_op jit(solution)/shard_map/ppermute | solution.py:583
  183.0 45.6 %inverse.1.inv_ref = f32[768,768]{1,0:T(8,128)} custom-call(s32[16]{0:T(128)} %get-tuple-element.158.offs_ref, s32[1]{0:T(128)} %bitcast.15.core_ref, f32[8,72,768]{2,1,0:T(8,128)} %get-tuple-element.159.own_ref, f32[8,72,768]{2,1,0:T(8,128)} %get-tuple-element.160.other_ref, f32[8,768]{1,0:T(8,128)} %broadcast_in_dim.119.var_ref), custom_call_target="tpu_custom_call" | custom-call | tf_op jit(solution)/shard_map/inverse/pallas_call | solution.py:162
  229.4 16.1 %update.1 = f32[1024,512]{1,0:T(8,128)} custom-call(s32[8]{0:T(128)} %get-tuple-element.155.roffs_ref, s32[16]{0:T(128)} %get-tuple-element.156.coffs_ref, s32[1]{0:T(128)} %bitcast.14.row_ref, s32[1]{0:T(128)} %bitcast.15.core_ref, f32[768,768]{1,0:T(8,128)} %inverse.1.inv_ref, f32[2,128,512]{2,1,0:T(8,128)} %get-tuple-element.161.x0, ...), custom_call_target="tpu_custom_call" | custom-call | tf_op jit(solution)/shard_map/update/pallas_call | solution.py:293
  (90 shorter events, 19.4 us)
Async XLA Ops:
  1.6 143.0 %copy-start.24 = (s32[16]{0:T(128)}, s32[16]{0:T(128)S(1)}, u32[]{:S(2)}) copy-start(s32[16]{0:T(128)S(1)} %get-tuple-element.508) | copy-start | bytes 196
  4.5 29.1 %copy-start.22 = (s32[8]{0:T(128)}, s32[8]{0:T(128)S(1)}, u32[]{:S(2)}) copy-start(s32[8]{0:T(128)S(1)} %get-tuple-element.457) | copy-start | bytes 100
  15.5 11.4 %all-to-all-start.9 = ((f32[8,72,128]{2,1,0:T(8,128)}), f32[8,72,128]{2,1,0:T(8,128)S(1)}, u32[]{:S(2)}, u32[]{:S(2)}) async-start(f32[8,72,128]{2,1,0:T(8,128)} %get-tuple-element.157), calls=%async_computation.9 | async-start | bytes 589824 | tf_op jit(solution)/shard_map/all_to_all | solution.py:507
  33.6 6.4 %copy-start.12 = (f32[72,1024]{1,0:T(8,128)S(1)}, f32[72,1024]{1,0:T(8,128)}, u32[]{:S(2)}) copy-start(f32[72,1024]{1,0:T(8,128)} %get-tuple-element.154.b_ref) | copy-start | bytes 884740
  33.6 14.1 %copy-start.11 = (f32[64,128]{1,0:T(8,128)S(1)}, f32[64,128]{1,0:T(8,128)}, u32[]{:S(2)}) copy-start(f32[64,128]{1,0:T(8,128)} %param.14) | copy-start | bytes 98308
  33.6 14.1 %copy-start.13 = (f32[2,64,128]{2,1,0:T(8,128)S(1)}, f32[2,64,128]{2,1,0:T(8,128)}, u32[]{:S(2)}) copy-start(f32[2,64,128]{2,1,0:T(8,128)} %param.13) | copy-start | bytes 196612
  33.7 33.1 %all-to-all-start.10 = ((f32[8,72,768]{2,1,0:T(8,128)}), f32[8,72,768]{2,1,0:T(8,128)}, u32[]{:S(2)}, u32[]{:S(2)}) async-start(f32[8,72,768]{2,1,0:T(8,128)} %widen.1), calls=%async_computation.10 | async-start | bytes 3538944 | tf_op jit(solution)/shard_map/all_to_all | solution.py:507
  40.0 22.2 %collective-permute-start.10 = (f32[72,256]{1,0:T(8,128)S(1)}, f32[72,256]{1,0:T(8,128)S(1)}, u32[]{:S(2)}, u32[]{:S(2)}) collective-permute-start(f32[72,256]{1,0:T(8,128)S(1)} %get-tuple-element.424), channel_id=1, source_target_pairs={{0,16},{16,32},{32,48},{48,64},{64,80},{80,96},{96,112},{1,17},{17... | collective-permute-start | bytes 221192 | tf_op jit(solution)/shard_map/ppermute | solution.py:490
  42.5 19.7 %collective-permute-start.11 = (f32[72,256]{1,0:T(8,128)S(1)}, f32[72,256]{1,0:T(8,128)S(1)}, u32[]{:S(2)}, u32[]{:S(2)}) collective-permute-start(f32[72,256]{1,0:T(8,128)S(1)} %get-tuple-element.423), channel_id=1, source_target_pairs={{16,0},{32,16},{48,32},{64,48},{80,64},{96,80},{112,96},{17,1},{33... | collective-permute-start | bytes 221192 | tf_op jit(solution)/shard_map/ppermute | solution.py:493
  52.1 14.6 %copy-start.5 = (f32[5,12,128]{2,1,0:T(8,128)}, f32[5,12,128]{2,1,0:T(8,128)S(1)}, u32[]{:S(2)}) copy-start(f32[5,12,128]{2,1,0:T(8,128)S(1)} %copy.92.w_ref) | copy-start | bytes 92164
  66.7 5.2 %copy-start = (f32[1024,512]{1,0:T(8,128)S(1)}, f32[1024,512]{1,0:T(8,128)}, u32[]{:S(2)}) copy-start(f32[1024,512]{1,0:T(8,128)} %b_ref.1) | copy-start | bytes 6291460
  66.7 113.1 %all-to-all-start.8 = ((f32[8,72,1024]{2,1,0:T(8,128)}), f32[8,72,1024]{2,1,0:T(8,128)}, u32[]{:S(2)}, u32[]{:S(2)}) async-start(f32[8,72,1024]{2,1,0:T(8,128)} %stencil_lanes.5), calls=%async_computation.8 | async-start | bytes 4718592 | tf_op jit(solution)/shard_map/all_to_all | solution.py:507
  72.0 35.1 %collective-permute-start.14 = (f32[256,512]{1,0:T(8,128)S(1)}, f32[256,512]{1,0:T(8,128)S(1)}, u32[]{:S(2)}, u32[]{:S(2)}) collective-permute-start(f32[256,512]{1,0:T(8,128)S(1)} %get-tuple-element.422), channel_id=1, source_target_pairs={{0,16},{16,32},{32,48},{48,64},{64,80},{80,96},{96,112},{1,17},{17... | collective-permute-start | bytes 1572872 | tf_op jit(solution)/shard_map/ppermute | solution.py:490
  75.5 43.1 %collective-permute-start.15 = (f32[256,512]{1,0:T(8,128)S(1)}, f32[256,512]{1,0:T(8,128)S(1)}, u32[]{:S(2)}, u32[]{:S(2)}) collective-permute-start(f32[256,512]{1,0:T(8,128)S(1)} %get-tuple-element.421), channel_id=1, source_target_pairs={{16,0},{32,16},{48,32},{64,48},{80,64},{96,80},{112,96},{17,1},{33... | collective-permute-start | bytes 1572872 | tf_op jit(solution)/shard_map/ppermute | solution.py:493
  79.7 102.7 %collective-permute-start.13 = (f32[8,72,768]{2,1,0:T(8,128)}, f32[8,72,768]{2,1,0:T(8,128)}, u32[]{:S(2)}, u32[]{:S(2)}) collective-permute-start(f32[8,72,768]{2,1,0:T(8,128)} %all-to-all-done.10), channel_id=1, source_target_pairs={{0,1},{1,0},{2,3},{3,2},{4,5},{5,4},{6,7},{7,6},{8,9},{9,8},{10,11... | collective-permute-start | bytes 5308424 | tf_op jit(solution)/shard_map/ppermute | solution.py:567
  107.1 11.5 %copy-start.15 = (f32[256,512]{1,0:T(8,128)}, f32[256,512]{1,0:T(8,128)S(1)}, u32[]{:S(2)}) copy-start(f32[256,512]{1,0:T(8,128)S(1)} %collective-permute-done.14.low_ref) | copy-start | bytes 1572868
  125.4 12.6 %copy-start.10 = (f32[128,512]{1,0:T(8,128)S(1)}, f32[128,512]{1,0:T(8,128)}, u32[]{:S(2)}) copy-start(f32[128,512]{1,0:T(8,128)} %get-tuple-element.153.b_ref) | copy-start | bytes 786436
  128.5 39.2 %collective-permute-start.16 = (f32[1024,256]{1,0:T(8,128)}, f32[1024,256]{1,0:T(8,128)}, u32[]{:S(2)}, u32[]{:S(2)}) collective-permute-start(f32[1024,256]{1,0:T(8,128)} %get-tuple-element.420), channel_id=1, source_target_pairs={{0,1},{1,2},{2,3},{3,4},{4,5},{5,6},{6,7},{7,8},{8,9},{9,10},{10,1... | collective-permute-start | bytes 3145736 | tf_op jit(solution)/shard_map/ppermute | solution.py:490
  136.0 33.3 %collective-permute-start.17 = (f32[1024,256]{1,0:T(8,128)}, f32[1024,256]{1,0:T(8,128)}, u32[]{:S(2)}, u32[]{:S(2)}) collective-permute-start(f32[1024,256]{1,0:T(8,128)} %get-tuple-element.419), channel_id=1, source_target_pairs={{1,0},{2,1},{3,2},{4,3},{5,4},{6,5},{7,6},{8,7},{9,8},{10,9},{11,1... | collective-permute-start | bytes 3145736 | tf_op jit(solution)/shard_map/ppermute | solution.py:493
  138.0 11.4 %collective-permute-start.4 = (f32[128,256]{1,0:T(8,128)S(1)}, f32[128,256]{1,0:T(8,128)S(1)}, u32[]{:S(2)}, u32[]{:S(2)}) collective-permute-start(f32[128,256]{1,0:T(8,128)S(1)} %get-tuple-element.426), channel_id=1, source_target_pairs={{0,1},{1,2},{2,3},{3,4},{4,5},{5,6},{6,7},{7,8},{8,9},{9,10},{10,1... | collective-permute-start | bytes 393224 | tf_op jit(solution)/shard_map/ppermute | solution.py:490
  141.6 12.1 %collective-permute-start.5 = (f32[128,256]{1,0:T(8,128)S(1)}, f32[128,256]{1,0:T(8,128)S(1)}, u32[]{:S(2)}, u32[]{:S(2)}) collective-permute-start(f32[128,256]{1,0:T(8,128)S(1)} %get-tuple-element.425), channel_id=1, source_target_pairs={{1,0},{2,1},{3,2},{4,3},{5,4},{6,5},{7,6},{8,7},{9,8},{10,9},{11,1... | collective-permute-start | bytes 393224 | tf_op jit(solution)/shard_map/ppermute | solution.py:493
  146.4 1.3 copy-start.23
  146.5 11.0 %copy-start.21 = (f32[64,128]{1,0:T(8,128)S(1)}, f32[64,128]{1,0:T(8,128)}, u32[]{:S(2)}) copy-start(f32[64,128]{1,0:T(8,128)} %param.15) | copy-start | bytes 98308
  149.3 4.4 %copy-start.17 = (f32[128,256]{1,0:T(8,128)}, f32[128,256]{1,0:T(8,128)S(1)}, u32[]{:S(2)}) copy-start(f32[128,256]{1,0:T(8,128)S(1)} %collective-permute-done.4.low_ref) | copy-start | bytes 393220
  156.6 8.7 %collective-permute-start.6 = (f32[128,512]{1,0:T(8,128)}, f32[128,512]{1,0:T(8,128)S(1)}, u32[]{:S(2)}, u32[]{:S(2)}) collective-permute-start(f32[128,512]{1,0:T(8,128)} %stencil_lanes.4), channel_id=1, source_target_pairs={{0,16},{16,0},{32,48},{48,32},{64,80},{80,64},{96,112},{112,96},{1... | collective-permute-start | bytes 786440 | tf_op jit(solution)/shard_map/ppermute | solution.py:577
  166.3 13.5 %copy-start.4 = (f32[2,128,512]{2,1,0:T(8,128)}, f32[2,128,512]{2,1,0:T(8,128)S(1)}, u32[]{:S(2)}) copy-start(f32[2,128,512]{2,1,0:T(8,128)S(1)} %pad_maximum_fusion) | copy-start | bytes 1572868
  166.3 62.3 %collective-permute-start.7 = (f32[2,128,512]{2,1,0:T(8,128)S(1)}, f32[2,128,512]{2,1,0:T(8,128)S(1)}, u32[]{:S(2)}, u32[]{:S(2)}) collective-permute-start(f32[2,128,512]{2,1,0:T(8,128)S(1)} %pad_maximum_fusion), channel_id=1, source_target_pairs={{0,32},{16,48},{32,64},{48,80},{64,96},{80,112},{96,0},{112,16},{1... | collective-permute-start | bytes 1572872 | tf_op jit(solution)/shard_map/ppermute | solution.py:579
  166.4 62.3 %collective-permute-start.8 = (f32[2,128,512]{2,1,0:T(8,128)S(1)}, f32[2,128,512]{2,1,0:T(8,128)}, u32[]{:S(2)}, u32[]{:S(2)}) collective-permute-start(f32[2,128,512]{2,1,0:T(8,128)S(1)} %pad_maximum_fusion), channel_id=1, source_target_pairs={{0,64},{16,80},{32,96},{48,112},{64,0},{80,16},{96,32},{112,48},{1... | collective-permute-start | bytes 1572872 | tf_op jit(solution)/shard_map/ppermute | solution.py:579
  167.7 60.9 %collective-permute-start.9 = (f32[2,128,512]{2,1,0:T(8,128)S(1)}, f32[2,128,512]{2,1,0:T(8,128)}, u32[]{:S(2)}, u32[]{:S(2)}) collective-permute-start(f32[2,128,512]{2,1,0:T(8,128)S(1)} %pad_maximum_fusion), channel_id=1, source_target_pairs={{0,96},{16,112},{32,0},{48,16},{64,32},{80,48},{96,64},{112,80},{1... | collective-permute-start | bytes 1572872 | tf_op jit(solution)/shard_map/ppermute | solution.py:579
  179.8 48.9 %collective-permute-start.12 = (f32[8,72,1024]{2,1,0:T(8,128)}, f32[8,72,1024]{2,1,0:T(8,128)}, u32[]{:S(2)}, u32[]{:S(2)}) collective-permute-start(f32[8,72,1024]{2,1,0:T(8,128)} %all-to-all-done.8), channel_id=1, source_target_pairs={{0,1},{1,0},{2,3},{3,2},{4,5},{5,4},{6,7},{7,6},{8,9},{9,8},{10,11... | collective-permute-start | bytes 7077896 | tf_op jit(solution)/shard_map/ppermute | solution.py:583
  183.0 46.4 %copy-start.6 = (f32[5,12,128]{2,1,0:T(8,128)S(1)}, f32[5,12,128]{2,1,0:T(8,128)}, u32[]{:S(2)}) copy-start(f32[5,12,128]{2,1,0:T(8,128)} %copy-done.5) | copy-start | bytes 92164
  228.6 0.8 copy-start.14
  (5 other events, 3.5 us)
where the time goes:
time: 246 us
  Pallas kernels  95.1 us (39%)
  starting transfers between devices  60 us (24%)
  waiting for transfers between devices  59.8 us (24%)
  local copies, waits for them, and re-layouts  19.6 us (8%)
  between operations  5.67 us (2%)
  other arithmetic  5.42 us (2%)
    pallas_call x1, Pallas kernels, inverse(): pl.pallas_call(functools.partial(inverse_kernel, n=n, cap=cap), out_shape...  45.6 us
    ppermute x4, waiting for transfers between devices, halos(): lax.ppermute(lax.slice_in_dim(block, block.shape[dim] - width, None, axis...  32.2 us
    all_to_all x3, starting transfers between devices, share(): return lax.all_to_all(copies, axis, 0, 0, axis_index_groups=groups)  17.3 us
    ppermute x4, starting transfers between devices, halos(): lax.ppermute(lax.slice_in_dim(block, block.shape[dim] - width, None, axis...  17.1 us
    pallas_call x1, Pallas kernels, final(): pl.pallas_call(final_kernel, out_shape=jax.ShapeDtypeStruct(prior.shape,...  16.1 us
    ppermute x4, waiting for transfers between devices, halos(): lax.ppermute(lax.slice_in_dim(block, 0, width, axis=dim), axis, backward)  15.9 us
    ppermute x4, starting transfers between devices, halos(): lax.ppermute(lax.slice_in_dim(block, 0, width, axis=dim), axis, backward)  14.3 us
    pallas_call x1, Pallas kernels, prior_cols(): pl.pallas_call(prior_kernel, out_shape=jax.ShapeDtypeStruct(block.shape,...  10.5 us
  transfers between devices with their start and end apart: 17, of which 7 were waited for; matrix products, arithmetic and copies ran while one was open for 6% of the time, Pallas kernels for 27%

commit v1 on v0

--- a/solution.py
+++ b/solution.py
@@ -255,10 +255,7 @@
     )(slots[:, :, None], pieces)
 
 
-def final_kernel(
-    roffs_ref, coffs_ref, row_ref, core_ref, inv_ref, x0, x1, x2, x3, own_ref, other_ref, prior_ref,
-    o_ref, xs_ref, ys_ref, gain_ref,
-):
+def gain_kernel(offs_ref, row_ref, inv_ref, x0, x1, x2, x3, o_ref, xs_ref):
     n = inv_ref.shape[0]
     pairs = (x0, x1, x2, x3)
     row = row_ref[0]
@@ -269,14 +266,31 @@
             @pl.when((row // 2 - b) % len(pairs) == k)
             def _():
                 for h in range(2):
-                    at = pl.ds(roffs_ref[2 * b + h], pair.shape[1])
+                    at = pl.ds(offs_ref[2 * b + h], pair.shape[1])
                     put_rows(xs_ref, at, pair, (row - h) % 2)
 
         return carry
 
     lax.fori_loop(0, len(pairs), pack, 0)
-    pack_pairs(core_ref[0], coffs_ref, own_ref, other_ref, ys_ref, own_ref.shape[1])
-    gain_ref[...] = dot(inv_ref[...], flat(xs_ref, slice(0, n)))
+    o_ref[...] = dot(inv_ref[...], flat(xs_ref, slice(0, n)))
+
+
+def gained(offs, row, inv, pairs):
+    n = inv.shape[0]
+    cap, cols = pairs[0].shape[1:]
+    return pl.pallas_call(
+        gain_kernel,
+        out_shape=jax.ShapeDtypeStruct((n, cols), F32),
+        in_specs=[SM, SM] + [VM] * 5,
+        out_specs=VM,
+        scratch_shapes=[pltpu.VMEM((cols // W, n + cap, W), F32)],
+        name="gain",
+    )(offs, row, inv, *pairs)
+
+
+def final_kernel(offs_ref, core_ref, gain_ref, own_ref, other_ref, prior_ref, o_ref, ys_ref):
+    n = gain_ref.shape[0]
+    pack_pairs(core_ref[0], offs_ref, own_ref, other_ref, ys_ref, own_ref.shape[1])
     per = 2
 
     def body(g, carry):
@@ -288,20 +302,17 @@
     lax.fori_loop(0, o_ref.shape[0] // (per * W), body, 0)
 
 
-def final(roffs, coffs, row, core, inv, pairs, own, other, prior):
-    n = inv.shape[0]
+def final(offs, core, gain, own, other, prior):
     return pl.pallas_call(
         final_kernel,
         out_shape=jax.ShapeDtypeStruct(prior.shape, F32),
-        in_specs=[SM, SM, SM, SM] + [VM] * 8,
+        in_specs=[SM, SM] + [VM] * 4,
         out_specs=VM,
         scratch_shapes=[
-            pltpu.VMEM((prior.shape[1] // W, n + pairs[0].shape[1], W), F32),
-            pltpu.VMEM((prior.shape[0] // W, n + own.shape[1], W), F32),
-            pltpu.VMEM((n, prior.shape[1]), F32),
+            pltpu.VMEM((prior.shape[0] // W, gain.shape[0] + own.shape[1], W), F32),
         ],
         name="update",
-    )(roffs, coffs, row, core, inv, *pairs, own, other, prior)
+    )(offs, core, gain, own, other, prior)
 
 
 def stencil_table(wind, diffusivity):
@@ -603,11 +614,9 @@
         own, other = cores(gather_sum(picked(ordered - col_start, long_x()), "col"))
         return even_cols, own, other
 
-    def long_update():
+    def long_rows():
         x = long_x()
-        y = gather_sum(picked(ordered - col_start, cov), "col")
         x = twice_cols(col_w, x, *halos(x, "col", 1, margin))
-        y = twice_cols(row_w, y, *halos(y, "row", 1, margin))
         pieces = windows(x, CAP_ROW, ROWS).reshape((ROWS // 2, 2, CAP_ROW, -1))
         pieces = jnp.stack(
             [lax.dynamic_index_in_dim(pieces, (row + k) % 2, 1, keepdims=False) for k in range(2)], 1
@@ -616,7 +625,11 @@
             lax.dynamic_index_in_dim(pieces, (row // 2 - k) % (ROWS // 2), 0, keepdims=False)
             for k in range(ROWS // 2)
         )
-        return (even_rows, even_cols, sets) + cores(y)
+        return even_rows, sets
+
+    def long_cols():
+        y = gather_sum(picked(ordered - col_start, cov), "col")
+        return (even_cols,) + cores(twice_cols(row_w, y, *halos(y, "row", 1, margin)))
 
     def unless(fits, short, long):
         def body(state):
@@ -626,10 +639,10 @@
 
     c_offs, c_own, c_other = unless(fits, (col_offs, c_own, c_other), long_corner)
     inv = inverse(c_offs, core, c_own, c_other, variances)
-    x_offs, y_offs, pairs, y_own, y_other = unless(
-        fits, (row_offs, col_offs, pairs, y_own, y_other), long_update
-    )
-    return final(x_offs, y_offs, row[None], core, inv, pairs, y_own, y_other, prior)
+    x_offs, pairs = unless(fits, (row_offs, pairs), long_rows)
+    gain = gained(x_offs, row[None], inv, pairs)
+    y_offs, y_own, y_other = unless(fits, (col_offs, y_own, y_other), long_cols)
+    return final(y_offs, core, gain, y_own, y_other, prior)
 
 
 def solution(mesh):

time: 246 us -> 246 us (level)
  the two profiles are of different devices: /device:TPU:19 before, /device:TPU:101 now
where the time goes in v1:
time: 246 us; the launch traced here: 243 us
  Pallas kernels  95.4 us (39%)
  starting transfers between devices  65.6 us (27%)
  waiting for transfers between devices  52.1 us (21%)
  local copies, waits for them, and re-layouts  18.8 us (8%)
  between operations  5.53 us (2%)
  other arithmetic  5.36 us (2%)
    pallas_call x1, Pallas kernels, inverse(): pl.pallas_call(functools.partial(inverse_kernel, n=n, cap=cap), out_shape...  45.5 us
    ppermute x4, waiting for transfers between devices, halos(): lax.ppermute(lax.slice_in_dim(block, 0, width, axis=dim), axis, backward)  31.7 us
    ppermute x4, starting transfers between devices, halos(): lax.ppermute(lax.slice_in_dim(block, block.shape[dim] - width, None, axis...  16.9 us
    all_to_all x3, starting transfers between devices, share(): return lax.all_to_all(copies, axis, 0, 0, axis_index_groups=groups)  16.7 us
    ppermute x4, starting transfers between devices, halos(): lax.ppermute(lax.slice_in_dim(block, 0, width, axis=dim), axis, backward)  16.4 us
    pallas_call x1, Pallas kernels, final(): pl.pallas_call(final_kernel, out_shape=jax.ShapeDtypeStruct(prior.shape,...  11.3 us
    ppermute x4, waiting for transfers between devices, halos(): lax.ppermute(lax.slice_in_dim(block, block.shape[dim] - width, None, axis...  8.17 us
    pallas_call x1, Pallas kernels, prior_cols(): pl.pallas_call(prior_kernel, out_shape=jax.ShapeDtypeStruct(block.shape,...  8.08 us
  transfers between devices with their start and end apart: 17, of which 8 were waited for; matrix products, arithmetic and copies ran while one was open for 6% of the time, Pallas kernels for 30%

profile of v1, /device:TPU:101, one launch (start us, length us, event | category | flops | bytes accessed | tf_op | source)
XLA Modules:
  0.0 242.8 jit_solution(14219905072333732485)
XLA Ops:
  9.8 5.6 %select.63 = (f32[128,512]{1,0:T(8,128)}, f32[72,1024]{1,0:T(8,128)}, f32[8,72,128]{2,1,0:T(8,128)}) custom-call(s32[128]{0:T(128)} %fusion.65.ridx_ref, s32[72,1]{1,0:T(8,128)} %copy.90.cidx_ref, f32[1024,512]{1,0:T(8,128)} %b_ref.1), custom_call_target="tpu_custom_call" | custom-call | tf_op jit(solution)/shard_map/select/pallas_call | solution.py:222
  15.3 6.9 %all-to-all-start.9 = ((f32[8,72,128]{2,1,0:T(8,128)}), f32[8,72,128]{2,1,0:T(8,128)S(1)}, u32[]{:S(2)}, u32[]{:S(2)}) async-start(f32[8,72,128]{2,1,0:T(8,128)} %get-tuple-element.172), calls=%async_computation.9 | async-start | bytes 589824 | tf_op jit(solution)/shard_map/all_to_all | solution.py:518
  23.2 4.9 %all-to-all-done.9.p_ref = f32[8,72,128]{2,1,0:T(8,128)S(1)} async-done(((f32[8,72,128]{2,1,0:T(8,128)}), f32[8,72,128]{2,1,0:T(8,128)S(1)}, u32[]{:S(2)}, u32[]{:S(2)}) %all-to-all-start.9) | async-done | bytes 294944 | tf_op jit(solution)/shard_map/all_to_all | solution.py:518
  28.8 5.9 %widen.1 = f32[8,72,768]{2,1,0:T(8,128)} custom-call(s32[8,128,1]{2,1,0:T(8,128)} %add_select_fusion.slot_ref, f32[8,72,128]{2,1,0:T(8,128)} %copy-done.9), custom_call_target="tpu_custom_call" | custom-call | tf_op jit(solution)/shard_map/widen/pallas_call | solution.py:249
  34.8 4.7 %all-to-all-start.10 = ((f32[8,72,768]{2,1,0:T(8,128)}), f32[8,72,768]{2,1,0:T(8,128)}, u32[]{:S(2)}, u32[]{:S(2)}) async-start(f32[8,72,768]{2,1,0:T(8,128)} %widen.1), calls=%async_computation.10 | async-start | bytes 3538944 | tf_op jit(solution)/shard_map/all_to_all | solution.py:518
  39.5 3.7 %collective-permute-start.5 = (f32[72,256]{1,0:T(8,128)S(1)}, f32[72,256]{1,0:T(8,128)S(1)}, u32[]{:S(2)}, u32[]{:S(2)}) collective-permute-start(f32[72,256]{1,0:T(8,128)S(1)} %get-tuple-element.472), channel_id=1, source_target_pairs={{16,0},{32,16},{48,32},{64,48},{80,64},{96,80},{112,96},{17,1},{33... | collective-permute-start | bytes 221192 | tf_op jit(solution)/shard_map/ppermute | solution.py:504
  43.2 4.0 %collective-permute-start.4 = (f32[72,256]{1,0:T(8,128)S(1)}, f32[72,256]{1,0:T(8,128)S(1)}, u32[]{:S(2)}, u32[]{:S(2)}) collective-permute-start(f32[72,256]{1,0:T(8,128)S(1)} %get-tuple-element.473), channel_id=1, source_target_pairs={{0,16},{16,32},{32,48},{48,64},{64,80},{80,96},{96,112},{1,17},{17... | collective-permute-start | bytes 221192 | tf_op jit(solution)/shard_map/ppermute | solution.py:501
  47.4 2.7 %copy.89 = f32[5,64,128]{0,2,1:T(8,128)} copy(f32[5,64,128]{2,1,0:T(8,128)S(1)} %bitcast_dynamic-update-slice_fusion) | data formatting | bytes 327680 | tf_op jit(solution)/shard_map/stack | solution.py:329
  51.6 8.6 %collective-permute-done.5.high_ref = f32[72,256]{1,0:T(8,128)S(1)} collective-permute-done((f32[72,256]{1,0:T(8,128)S(1)}, f32[72,256]{1,0:T(8,128)S(1)}, u32[]{:S(2)}, u32[]{:S(2)}) %collective-permute-start.5) | collective-permute-done | bytes 73760 | tf_op jit(solution)/shard_map/ppermute | solution.py:504
  61.4 3.2 %stencil_lanes.4 = f32[8,72,1024]{2,1,0:T(8,128)} custom-call(f32[5,12,128]{2,1,0:T(8,128)S(1)} %copy.91.w_ref, f32[72,1024]{1,0:T(8,128)} %get-tuple-element.168.b_ref, f32[72,256]{1,0:T(8,128)} %copy-done.20, f32[72,256]{1,0:T(8,128)} %copy-done.19), custom_call_target="tpu_custom_call" | custom-call | tf_op jit(solution)/shard_map/stencil_lanes/pallas_call | solution.py:371
  64.7 5.1 %all-to-all-start.8 = ((f32[8,72,1024]{2,1,0:T(8,128)}), f32[8,72,1024]{2,1,0:T(8,128)}, u32[]{:S(2)}, u32[]{:S(2)}) async-start(f32[8,72,1024]{2,1,0:T(8,128)} %stencil_lanes.4), calls=%async_computation.8 | async-start | bytes 4718592 | tf_op jit(solution)/shard_map/all_to_all | solution.py:518
  69.9 3.4 %collective-permute-start.15 = (f32[256,512]{1,0:T(8,128)S(1)}, f32[256,512]{1,0:T(8,128)S(1)}, u32[]{:S(2)}, u32[]{:S(2)}) collective-permute-start(f32[256,512]{1,0:T(8,128)S(1)} %get-tuple-element.470), channel_id=1, source_target_pairs={{16,0},{32,16},{48,32},{64,48},{80,64},{96,80},{112,96},{17,1},{33... | collective-permute-start | bytes 1572872 | tf_op jit(solution)/shard_map/ppermute | solution.py:504
  73.3 4.2 %collective-permute-start.14 = (f32[256,512]{1,0:T(8,128)S(1)}, f32[256,512]{1,0:T(8,128)S(1)}, u32[]{:S(2)}, u32[]{:S(2)}) collective-permute-start(f32[256,512]{1,0:T(8,128)S(1)} %get-tuple-element.471), channel_id=1, source_target_pairs={{0,16},{16,32},{32,48},{48,64},{64,80},{80,96},{96,112},{1,17},{17... | collective-permute-start | bytes 1572872 | tf_op jit(solution)/shard_map/ppermute | solution.py:501
  77.6 5.5 %collective-permute-start.13 = (f32[8,72,768]{2,1,0:T(8,128)}, f32[8,72,768]{2,1,0:T(8,128)}, u32[]{:S(2)}, u32[]{:S(2)}) collective-permute-start(f32[8,72,768]{2,1,0:T(8,128)} %all-to-all-done.10), channel_id=1, source_target_pairs={{0,1},{1,0},{2,3},{3,2},{4,5},{5,4},{6,7},{7,6},{8,9},{9,8},{10,11... | collective-permute-start | bytes 5308424 | tf_op jit(solution)/shard_map/ppermute | solution.py:578
  83.1 2.1 fusion.74.w_ref.wr_ref
  85.2 21.7 %collective-permute-done.15.high_ref = f32[256,512]{1,0:T(8,128)S(1)} collective-permute-done((f32[256,512]{1,0:T(8,128)S(1)}, f32[256,512]{1,0:T(8,128)S(1)}, u32[]{:S(2)}, u32[]{:S(2)}) %collective-permute-start.15) | collective-permute-done | bytes 524320 | tf_op jit(solution)/shard_map/ppermute | solution.py:504
  106.9 6.4 %collective-permute-done.14.low_ref = f32[256,512]{1,0:T(8,128)S(1)} collective-permute-done((f32[256,512]{1,0:T(8,128)S(1)}, f32[256,512]{1,0:T(8,128)S(1)}, u32[]{:S(2)}, u32[]{:S(2)}) %collective-permute-start.14) | collective-permute-done | bytes 524320 | tf_op jit(solution)/shard_map/ppermute | solution.py:501
  114.1 5.9 %stencil_rows.1.b_ref = f32[1024,512]{1,0:T(8,128)} custom-call(f32[12,128,5]{2,1,0:T(8,128)} %fusion.74.w_ref.wr_ref, f32[1024,512]{1,0:T(8,128)S(1)} %copy-done, f32[256,512]{1,0:T(8,128)} %copy-done.16, f32[256,512]{1,0:T(8,128)} %copy-done.15), custom_call_target="tpu_custom_call" | custom-call | tf_op jit(solution)/shard_map/stencil_rows/pallas_call | solution.py:428
  120.0 3.1 %fusion.69 = (f32[1024,256]{1,0:T(8,128)}, f32[1024,256]{1,0:T(8,128)}) fusion(f32[1024,512]{1,0:T(8,128)} %stencil_rows.1.b_ref), kind=kLoop, calls=%fused_computation.170 | loop fusion | bytes 4194304 | tf_op jit(solution)/shard_map/slice | solution.py:504
  123.1 7.3 %collective-permute-start.17 = (f32[1024,256]{1,0:T(8,128)}, f32[1024,256]{1,0:T(8,128)}, u32[]{:S(2)}, u32[]{:S(2)}) collective-permute-start(f32[1024,256]{1,0:T(8,128)} %get-tuple-element.468), channel_id=1, source_target_pairs={{1,0},{2,1},{3,2},{4,3},{5,4},{6,5},{7,6},{8,7},{9,8},{10,9},{11,1... | collective-permute-start | bytes 3145736 | tf_op jit(solution)/shard_map/ppermute | solution.py:504
  130.4 3.0 %collective-permute-start.16 = (f32[1024,256]{1,0:T(8,128)}, f32[1024,256]{1,0:T(8,128)}, u32[]{:S(2)}, u32[]{:S(2)}) collective-permute-start(f32[1024,256]{1,0:T(8,128)} %get-tuple-element.469), channel_id=1, source_target_pairs={{0,1},{1,2},{2,3},{3,4},{4,5},{5,6},{6,7},{7,8},{8,9},{9,10},{10,1... | collective-permute-start | bytes 3145736 | tf_op jit(solution)/shard_map/ppermute | solution.py:501
  133.4 1.9 collective-permute-start.8
  135.4 5.8 %collective-permute-start.7 = (f32[128,256]{1,0:T(8,128)S(1)}, f32[128,256]{1,0:T(8,128)S(1)}, u32[]{:S(2)}, u32[]{:S(2)}) collective-permute-start(f32[128,256]{1,0:T(8,128)S(1)} %get-tuple-element.475), channel_id=1, source_target_pairs={{0,1},{1,2},{2,3},{3,4},{4,5},{5,6},{6,7},{7,8},{8,9},{9,10},{10,1... | collective-permute-start | bytes 393224 | tf_op jit(solution)/shard_map/ppermute | solution.py:501
  147.4 2.2 stencil_lanes.5
  150.6 7.2 %collective-permute-done.9 = f32[128,512]{1,0:T(8,128)S(1)} collective-permute-done((f32[128,512]{1,0:T(8,128)}, f32[128,512]{1,0:T(8,128)S(1)}, u32[]{:S(2)}, u32[]{:S(2)}) %collective-permute-start.9) | collective-permute-done | bytes 262176 | tf_op jit(solution)/shard_map/ppermute | solution.py:588
  158.8 4.9 %collective-permute-start.12 = (f32[2,128,512]{2,1,0:T(8,128)S(1)}, f32[2,128,512]{2,1,0:T(8,128)S(1)}, u32[]{:S(2)}, u32[]{:S(2)}) collective-permute-start(f32[2,128,512]{2,1,0:T(8,128)S(1)} %pad_maximum_fusion), channel_id=1, source_target_pairs={{0,96},{16,112},{32,0},{48,16},{64,32},{80,48},{96,64},{112,80},{1... | collective-permute-start | bytes 1572872 | tf_op jit(solution)/shard_map/ppermute | solution.py:590
  163.7 2.2 collective-permute-start.11
  166.3 8.1 %prior_lanes.1.prior_ref = f32[1024,512]{1,0:T(8,128)} custom-call(s32[1]{0:T(128)} %bitcast.16.gap_ref, f32[5,8,128]{2,1,0:T(8,128)S(1)} %copy.93.w_ref, f32[12,128,5]{2,1,0:T(8,128)} %fusion.74.w_ref.wr_ref, f32[8,128]{1,0:T(8,128)} %pad_dynamic-slice_fusion.10.noise_ref, f32[1024,512]{1,0:T(8,128)} %stencil_rows.1.b_ref, ...), custom_call_target="tpu_custom_call" | custom-call | tf_op jit(solution)/shard_map/prior_lanes/pallas_call | solution.py:487
  174.4 2.5 %collective-permute-start.6 = (f32[8,72,1024]{2,1,0:T(8,128)}, f32[8,72,1024]{2,1,0:T(8,128)}, u32[]{:S(2)}, u32[]{:S(2)}) collective-permute-start(f32[8,72,1024]{2,1,0:T(8,128)} %all-to-all-done.8), channel_id=1, source_target_pairs={{0,1},{1,0},{2,3},{3,2},{4,5},{5,4},{6,7},{7,6},{8,9},{9,8},{10,11... | collective-permute-start | bytes 7077896 | tf_op jit(solution)/shard_map/ppermute | solution.py:594
  177.5 45.5 %inverse.1.inv_ref = f32[768,768]{1,0:T(8,128)} custom-call(s32[16]{0:T(128)} %get-tuple-element.173.offs_ref, s32[1]{0:T(128)} %bitcast.12.core_ref, f32[8,72,768]{2,1,0:T(8,128)} %get-tuple-element.174.own_ref, f32[8,72,768]{2,1,0:T(8,128)} %get-tuple-element.175.other_ref, f32[8,768]{1,0:T(8,128)} %broadcast_in_dim.119.var_ref), custom_call_target="tpu_custom_call" | custom-call | tf_op jit(solution)/shard_map/inverse/pallas_call | solution.py:162
  223.9 7.5 %gain.1.gain_ref = f32[768,512]{1,0:T(8,128)} custom-call(s32[8]{0:T(128)} %get-tuple-element.171.offs_ref, s32[1]{0:T(128)} %bitcast.15.row_ref, f32[768,768]{1,0:T(8,128)} %inverse.1.inv_ref, f32[2,128,512]{2,1,0:T(8,128)} %get-tuple-element.176.x0, f32[2,128,512]{2,1,0:T(8,128)} %get-tuple-element.177.x1, f32[2,128,512]{2,1,0:T(8,128)} %get-tuple-element.178.x2, ...), custom_call_target="tpu_custom_call" | custom-call | tf_op jit(solution)/shard_map/gain/pallas_call | solution.py:281
  231.4 11.3 %update.1 = f32[1024,512]{1,0:T(8,128)} custom-call(s32[16]{0:T(128)} %get-tuple-element.169.offs_ref, s32[1]{0:T(128)} %bitcast.12.core_ref, f32[768,512]{1,0:T(8,128)} %gain.1.gain_ref, f32[8,72,1024]{2,1,0:T(8,128)} %get-tuple-element.180.own_ref, f32[8,72,1024]{2,1,0:T(8,128)} %get-tuple-element.181.other_ref, f32[1024,512]{1,0:T(8,128)} %prior_lanes.1.prior_ref), custom_call_target="tpu_custom_call" | custom-call | tf_op jit(solution)/shard_map/update/pallas_call | solution.py:306
  (92 shorter events, 20.0 us)
Async XLA Ops:
  1.7 139.4 %copy-start.24 = (s32[16]{0:T(128)}, s32[16]{0:T(128)S(1)}, u32[]{:S(2)}) copy-start(s32[16]{0:T(128)S(1)} %get-tuple-element.569) | copy-start | bytes 196
  4.4 30.4 %copy-start.22 = (s32[8]{0:T(128)}, s32[8]{0:T(128)S(1)}, u32[]{:S(2)}) copy-start(s32[8]{0:T(128)S(1)} %get-tuple-element.536) | copy-start | bytes 100
  15.3 12.7 %all-to-all-start.9 = ((f32[8,72,128]{2,1,0:T(8,128)}), f32[8,72,128]{2,1,0:T(8,128)S(1)}, u32[]{:S(2)}, u32[]{:S(2)}) async-start(f32[8,72,128]{2,1,0:T(8,128)} %get-tuple-element.172), calls=%async_computation.9 | async-start | bytes 589824 | tf_op jit(solution)/shard_map/all_to_all | solution.py:518
  34.8 4.7 %copy-start.12 = (f32[72,1024]{1,0:T(8,128)S(1)}, f32[72,1024]{1,0:T(8,128)}, u32[]{:S(2)}) copy-start(f32[72,1024]{1,0:T(8,128)} %get-tuple-element.168.b_ref) | copy-start | bytes 884740
  34.8 12.5 %copy-start.11 = (f32[64,128]{1,0:T(8,128)S(1)}, f32[64,128]{1,0:T(8,128)}, u32[]{:S(2)}) copy-start(f32[64,128]{1,0:T(8,128)} %param.16) | copy-start | bytes 98308
  34.8 12.5 %copy-start.13 = (f32[2,64,128]{2,1,0:T(8,128)S(1)}, f32[2,64,128]{2,1,0:T(8,128)}, u32[]{:S(2)}) copy-start(f32[2,64,128]{2,1,0:T(8,128)} %param.15) | copy-start | bytes 196612
  34.8 29.9 %all-to-all-start.10 = ((f32[8,72,768]{2,1,0:T(8,128)}), f32[8,72,768]{2,1,0:T(8,128)}, u32[]{:S(2)}, u32[]{:S(2)}) async-start(f32[8,72,768]{2,1,0:T(8,128)} %widen.1), calls=%async_computation.10 | async-start | bytes 3538944 | tf_op jit(solution)/shard_map/all_to_all | solution.py:518
  39.5 20.7 %collective-permute-start.5 = (f32[72,256]{1,0:T(8,128)S(1)}, f32[72,256]{1,0:T(8,128)S(1)}, u32[]{:S(2)}, u32[]{:S(2)}) collective-permute-start(f32[72,256]{1,0:T(8,128)S(1)} %get-tuple-element.472), channel_id=1, source_target_pairs={{16,0},{32,16},{48,32},{64,48},{80,64},{96,80},{112,96},{17,1},{33... | collective-permute-start | bytes 221192 | tf_op jit(solution)/shard_map/ppermute | solution.py:504
  43.2 17.6 %collective-permute-start.4 = (f32[72,256]{1,0:T(8,128)S(1)}, f32[72,256]{1,0:T(8,128)S(1)}, u32[]{:S(2)}, u32[]{:S(2)}) collective-permute-start(f32[72,256]{1,0:T(8,128)S(1)} %get-tuple-element.473), channel_id=1, source_target_pairs={{0,16},{16,32},{32,48},{48,64},{64,80},{80,96},{96,112},{1,17},{17... | collective-permute-start | bytes 221192 | tf_op jit(solution)/shard_map/ppermute | solution.py:501
  51.6 9.2 %copy-start.7 = (f32[5,12,128]{2,1,0:T(8,128)}, f32[5,12,128]{2,1,0:T(8,128)S(1)}, u32[]{:S(2)}) copy-start(f32[5,12,128]{2,1,0:T(8,128)S(1)} %copy.91.w_ref) | copy-start | bytes 92164
  64.7 5.1 %copy-start = (f32[1024,512]{1,0:T(8,128)S(1)}, f32[1024,512]{1,0:T(8,128)}, u32[]{:S(2)}) copy-start(f32[1024,512]{1,0:T(8,128)} %b_ref.1) | copy-start | bytes 6291460
  64.7 109.7 %all-to-all-start.8 = ((f32[8,72,1024]{2,1,0:T(8,128)}), f32[8,72,1024]{2,1,0:T(8,128)}, u32[]{:S(2)}, u32[]{:S(2)}) async-start(f32[8,72,1024]{2,1,0:T(8,128)} %stencil_lanes.4), calls=%async_computation.8 | async-start | bytes 4718592 | tf_op jit(solution)/shard_map/all_to_all | solution.py:518
  69.9 37.1 %collective-permute-start.15 = (f32[256,512]{1,0:T(8,128)S(1)}, f32[256,512]{1,0:T(8,128)S(1)}, u32[]{:S(2)}, u32[]{:S(2)}) collective-permute-start(f32[256,512]{1,0:T(8,128)S(1)} %get-tuple-element.470), channel_id=1, source_target_pairs={{16,0},{32,16},{48,32},{64,48},{80,64},{96,80},{112,96},{17,1},{33... | collective-permute-start | bytes 1572872 | tf_op jit(solution)/shard_map/ppermute | solution.py:504
  73.3 40.0 %collective-permute-start.14 = (f32[256,512]{1,0:T(8,128)S(1)}, f32[256,512]{1,0:T(8,128)S(1)}, u32[]{:S(2)}, u32[]{:S(2)}) collective-permute-start(f32[256,512]{1,0:T(8,128)S(1)} %get-tuple-element.471), channel_id=1, source_target_pairs={{0,16},{16,32},{32,48},{48,64},{64,80},{80,96},{96,112},{1,17},{17... | collective-permute-start | bytes 1572872 | tf_op jit(solution)/shard_map/ppermute | solution.py:501
  77.6 99.3 %collective-permute-start.13 = (f32[8,72,768]{2,1,0:T(8,128)}, f32[8,72,768]{2,1,0:T(8,128)}, u32[]{:S(2)}, u32[]{:S(2)}) collective-permute-start(f32[8,72,768]{2,1,0:T(8,128)} %all-to-all-done.10), channel_id=1, source_target_pairs={{0,1},{1,0},{2,3},{3,2},{4,5},{5,4},{6,7},{7,6},{8,9},{9,8},{10,11... | collective-permute-start | bytes 5308424 | tf_op jit(solution)/shard_map/ppermute | solution.py:578
  106.9 6.4 %copy-start.15 = (f32[256,512]{1,0:T(8,128)}, f32[256,512]{1,0:T(8,128)S(1)}, u32[]{:S(2)}) copy-start(f32[256,512]{1,0:T(8,128)S(1)} %collective-permute-done.15.high_ref) | copy-start | bytes 1572868
  113.3 0.8 copy-start.16
  120.0 13.4 %copy-start.10 = (f32[128,512]{1,0:T(8,128)S(1)}, f32[128,512]{1,0:T(8,128)}, u32[]{:S(2)}) copy-start(f32[128,512]{1,0:T(8,128)} %get-tuple-element.170.b_ref) | copy-start | bytes 786436
  120.0 22.9 %copy-start.23 = (f32[3,256]{1,0:T(4,128)S(1)}, f32[3,256]{1,0:T(4,128)}, u32[]{:S(2)}) copy-start(f32[3,256]{1,0:T(4,128)} %param.14) | copy-start | bytes 9220
  123.1 42.8 %collective-permute-start.17 = (f32[1024,256]{1,0:T(8,128)}, f32[1024,256]{1,0:T(8,128)}, u32[]{:S(2)}, u32[]{:S(2)}) collective-permute-start(f32[1024,256]{1,0:T(8,128)} %get-tuple-element.468), channel_id=1, source_target_pairs={{1,0},{2,1},{3,2},{4,3},{5,4},{6,5},{7,6},{8,7},{9,8},{10,9},{11,1... | collective-permute-start | bytes 3145736 | tf_op jit(solution)/shard_map/ppermute | solution.py:504
  130.4 35.9 %collective-permute-start.16 = (f32[1024,256]{1,0:T(8,128)}, f32[1024,256]{1,0:T(8,128)}, u32[]{:S(2)}, u32[]{:S(2)}) collective-permute-start(f32[1024,256]{1,0:T(8,128)} %get-tuple-element.469), channel_id=1, source_target_pairs={{0,1},{1,2},{2,3},{3,4},{4,5},{5,6},{6,7},{7,8},{8,9},{9,10},{10,1... | collective-permute-start | bytes 3145736 | tf_op jit(solution)/shard_map/ppermute | solution.py:501
  133.4 12.1 %collective-permute-start.8 = (f32[128,256]{1,0:T(8,128)S(1)}, f32[128,256]{1,0:T(8,128)S(1)}, u32[]{:S(2)}, u32[]{:S(2)}) collective-permute-start(f32[128,256]{1,0:T(8,128)S(1)} %get-tuple-element.474), channel_id=1, source_target_pairs={{1,0},{2,1},{3,2},{4,3},{5,4},{6,5},{7,6},{8,7},{9,8},{10,9},{11,1... | collective-permute-start | bytes 393224 | tf_op jit(solution)/shard_map/ppermute | solution.py:504
  135.4 11.4 %collective-permute-start.7 = (f32[128,256]{1,0:T(8,128)S(1)}, f32[128,256]{1,0:T(8,128)S(1)}, u32[]{:S(2)}, u32[]{:S(2)}) collective-permute-start(f32[128,256]{1,0:T(8,128)S(1)} %get-tuple-element.475), channel_id=1, source_target_pairs={{0,1},{1,2},{2,3},{3,4},{4,5},{5,6},{6,7},{7,8},{8,9},{9,10},{10,1... | collective-permute-start | bytes 393224 | tf_op jit(solution)/shard_map/ppermute | solution.py:501
  142.9 6.8 %copy-start.21 = (f32[64,128]{1,0:T(8,128)S(1)}, f32[64,128]{1,0:T(8,128)}, u32[]{:S(2)}) copy-start(f32[64,128]{1,0:T(8,128)} %param.17) | copy-start | bytes 98308
  145.6 1.2 copy-start.17
  149.6 8.2 %collective-permute-start.9 = (f32[128,512]{1,0:T(8,128)}, f32[128,512]{1,0:T(8,128)S(1)}, u32[]{:S(2)}, u32[]{:S(2)}) collective-permute-start(f32[128,512]{1,0:T(8,128)} %stencil_lanes.5), channel_id=1, source_target_pairs={{0,16},{16,0},{32,48},{48,32},{64,80},{80,64},{96,112},{112,96},{1... | collective-permute-start | bytes 786440 | tf_op jit(solution)/shard_map/ppermute | solution.py:588
  158.8 15.6 %copy-start.6 = (f32[2,128,512]{2,1,0:T(8,128)}, f32[2,128,512]{2,1,0:T(8,128)S(1)}, u32[]{:S(2)}) copy-start(f32[2,128,512]{2,1,0:T(8,128)S(1)} %pad_maximum_fusion) | copy-start | bytes 1572868
  158.8 64.3 %collective-permute-start.12 = (f32[2,128,512]{2,1,0:T(8,128)S(1)}, f32[2,128,512]{2,1,0:T(8,128)S(1)}, u32[]{:S(2)}, u32[]{:S(2)}) collective-permute-start(f32[2,128,512]{2,1,0:T(8,128)S(1)} %pad_maximum_fusion), channel_id=1, source_target_pairs={{0,96},{16,112},{32,0},{48,16},{64,32},{80,48},{96,64},{112,80},{1... | collective-permute-start | bytes 1572872 | tf_op jit(solution)/shard_map/ppermute | solution.py:590
  163.7 59.4 %collective-permute-start.11 = (f32[2,128,512]{2,1,0:T(8,128)S(1)}, f32[2,128,512]{2,1,0:T(8,128)}, u32[]{:S(2)}, u32[]{:S(2)}) collective-permute-start(f32[2,128,512]{2,1,0:T(8,128)S(1)} %pad_maximum_fusion), channel_id=1, source_target_pairs={{0,64},{16,80},{32,96},{48,112},{64,0},{80,16},{96,32},{112,48},{1... | collective-permute-start | bytes 1572872 | tf_op jit(solution)/shard_map/ppermute | solution.py:590
  165.9 57.2 %collective-permute-start.10 = (f32[2,128,512]{2,1,0:T(8,128)S(1)}, f32[2,128,512]{2,1,0:T(8,128)}, u32[]{:S(2)}, u32[]{:S(2)}) collective-permute-start(f32[2,128,512]{2,1,0:T(8,128)S(1)} %pad_maximum_fusion), channel_id=1, source_target_pairs={{0,32},{16,48},{32,64},{48,80},{64,96},{80,112},{96,0},{112,16},{1... | collective-permute-start | bytes 1572872 | tf_op jit(solution)/shard_map/ppermute | solution.py:590
  174.4 57.0 %collective-permute-start.6 = (f32[8,72,1024]{2,1,0:T(8,128)}, f32[8,72,1024]{2,1,0:T(8,128)}, u32[]{:S(2)}, u32[]{:S(2)}) collective-permute-start(f32[8,72,1024]{2,1,0:T(8,128)} %all-to-all-done.8), channel_id=1, source_target_pairs={{0,1},{1,0},{2,3},{3,2},{4,5},{5,4},{6,7},{7,6},{8,9},{9,8},{10,11... | collective-permute-start | bytes 7077896 | tf_op jit(solution)/shard_map/ppermute | solution.py:594
  223.9 7.5 %copy-start.8 = (f32[5,12,128]{2,1,0:T(8,128)S(1)}, f32[5,12,128]{2,1,0:T(8,128)}, u32[]{:S(2)}) copy-start(f32[5,12,128]{2,1,0:T(8,128)} %copy-done.7) | copy-start | bytes 92164
  (5 other events, 3.4 us)
